TPU v7x, 128 devices: a whole 4x4x4 slice. The times are simulated.
128 devices in a mesh: row: 8 (over y, core), col: 16 (over z, x).
Axes of the slice: x: 4, y: 4, z: 4, core: 2. Of those that a mesh axis runs over, the one named last changes fastest.
Arguments:
- chol_window: bfloat16 [48, 48, 1536], P(None, None, ('row', 'col')), may hold values from -0.3125 to 0.3125
- chol_pairs: bfloat16 [512, 512, 1536], P('row', 'col'), may hold values from -0.3125 to 0.3125
- amplitudes: bfloat16 [48, 512, 1024], P(None, 'col', 'row'), may hold values from -6 to 6
- eps_window: float32 [48], P('col'), may hold values from 0.5 to 2
- eps_virtual: float32 [512], P('row'), may hold values from 0.5 to 2
- eps_occupied: float32 [1024], replicated, may hold values from 0.5 to 2
- dress_first: bfloat16 [1024, 1024], replicated, may hold values from -0.1875 to 0.1875
- dress_second: bfloat16 [1024, 1024], replicated, may hold values from -0.1875 to 0.1875
Outputs:
- resid: bfloat16 [48, 512, 1024], P('col', None, 'row')
All inputs are finite; a program needn't handle non-finite values.
Results may differ from a plain program's by a relative error of at most 0.0061.
Values may be sent and summed in bfloat16 or wider, within the bound.
No kernel may reach another device: no remote copies, remote signals or barrier semaphores. Data moves between devices by JAX's collectives and lax.ppermute only.
A program may use at most 192 MiB of HBM per device.

v0:
```python
import jax
import jax.numpy as jnp
from jax import lax
from jax.sharding import PartitionSpec as P


def local(
    chol_window,
    chol_pairs,
    amplitudes,
    eps_window,
    eps_virtual,
    eps_occupied,
    dress_first,
    dress_second,
):
    window = lax.all_gather(chol_window, ("row", "col"), axis=2, tiled=True)
    block_b, block_d, aux_count = chol_pairs.shape
    window_size = window.shape[0]
    groups = window_size // 8
    window_blocks = window.reshape(groups, 8, window_size, aux_count)

    def build_tile(block_index):
        slab = lax.dynamic_index_in_dim(window_blocks, block_index, 0, keepdims=False)
        values = jnp.einsum("acq,bdq->abcd", slab, chol_pairs, preferred_element_type=jnp.float32)
        return values.astype(jnp.bfloat16)

    integrals = lax.map(build_tile, jnp.arange(groups, dtype=jnp.int32))
    integrals = integrals.reshape(window_size, block_b, window_size, block_d)
    partial_value = jnp.einsum(
        "abcd,cdo->abo",
        integrals,
        lax.all_gather(amplitudes, "row", axis=2, tiled=True),
        preferred_element_type=jnp.float32,
    )
    summed = lax.psum_scatter(partial_value, "col", scatter_dimension=0, tiled=True)
    rows_a = summed.shape[0]
    occ_count = summed.shape[2]
    denominator = (
        eps_window[:, None, None] + eps_virtual[None, :, None] + eps_occupied[None, None, :]
    )
    scaled = (summed / denominator).astype(jnp.bfloat16)
    flattened = scaled.reshape(rows_a * block_b, occ_count)
    first_mix = jnp.dot(flattened, dress_first, preferred_element_type=jnp.float32).astype(
        jnp.bfloat16
    )
    mixed = flattened.astype(jnp.float32) + jnp.dot(
        first_mix, dress_second, preferred_element_type=jnp.float32
    )
    mixed = mixed.astype(jnp.bfloat16).reshape(rows_a, block_b, occ_count)
    return lax.all_to_all(mixed, "row", split_axis=2, concat_axis=1, tiled=True)


def solution(mesh):
    return jax.shard_map(
        local,
        mesh=mesh,
        in_specs=(
            P(None, None, ("row", "col")),
            P("row", "col", None),
            P(None, "col", "row"),
            P("col"),
            P("row"),
            P(),
            P(),
            P(),
        ),
        out_specs=P("col", None, "row"),
        check_vma=False,
    )
```

profile of v0, /device:TPU:1, one launch (start us, length us, event | category | flops | bytes accessed | tf_op | source)
XLA Modules:
  0.0 322.5 jit_solution(2280201207964700690)
XLA Ops:
  6.5 0.0 copy-start
  6.5 0.0 all-gather.3.cloned.1.call-start
  6.5 0.7 all-gather.3.cloned.1.call-update
  7.3 0.0 all-gather.5.cloned.1.call-start
  7.3 1.9 copy.15
  9.2 0.0 all-gather.5.cloned.1.call-update
  9.2 0.0 reduce-scatter.4.cloned.1.call-start
  9.3 8.9 %copy.14 = bf16[64,32,1536]{2,0,1:T(8,128)(2,1)} copy(bf16[64,32,1536]{2,1,0:T(8,128)(2,1)} %param.11) | data formatting | bytes 12582912 | tf_op jit(solution)/shard_map/while | solution.py:28
  18.2 78.6 %all-gather.3.cloned.1.call-done = bf16[48,48,1536]{1,0,2:T(8,128)(2,1)} async-done(((bf16[48,48,12]{1,0,2:T(8,128)(2,1)}), bf16[48,48,1536]{1,0,2:T(8,128)(2,1)}) %all-gather.3.cloned.1.call-update) | async-done | bytes 7077904 | tf_op jit(solution)/shard_map/all_gather | solution.py:17
  96.8 20.1 %copy.13 = bf16[6,8,48,1536]{3,2,1,0:T(8,128)(2,1)} copy(bf16[6,8,48,1536]{2,1,0,3:T(8,128)(2,1)} %bitcast.46) | data formatting | bytes 14155776 | tf_op jit(solution)/shard_map/while | solution.py:28
  116.9 65.8 %while.10 = (s32[]{:T(128)}, bf16[6,8,64,48,32]{2,3,4,1,0:T(8,128)(2,1)}, s32[6]{0:T(128)S(1)}, bf16[6,8,48,1536]{3,2,1,0:T(8,128)(2,1)}, bf16[64,32,1536]{2,0,1...) while((s32[]{:T(128)}, bf16[6,8,64,48,32]{2,3,4,1,0:T(8,128)(2,1)}, s32[6]{0:T(128)S(1)}, ...), condition=%wide.region_1.2_spmd, body=%wide.region_0.1_spmd.sunk | while | flops 2416705536 | bytes 10617479 | solution.py:28
  116.9 0.6 dynamic_slice.15
  119.2 8.6 %bitcast_dynamic-update-slice_fusion.2 = bf16[6,8,64,48,32]{2,3,4,1,0:T(8,128)(2,1)} fusion(bf16[6,8,64,48,32]{2,3,4,1,0:T(8,128)(2,1)} %get-tuple-element.93, s32[]{:T(128)} %get-tuple-element.92, bf16[64,32,1536]{2,0,1:T(8,128)(2,1)} %get-tuple-element.104, bf16[6,8,48,1536]{3,2,1,0:T(8,128)(2,1)} %get-tuple-element.103, s32[]{:T(128)S(6)} %select_n.5), kind=kOutput, calls=%fused_computation.2.clone.1 | convolution fusion | flops 2416705536 | bytes 10617348 | tf_op jit(solution)/shard_map/while/body/eval_jaxpr/acq,bdq->abcd/dot_general | solution.py:25
  127.8 0.6 dynamic_slice.15
  130.1 8.6 %bitcast_dynamic-update-slice_fusion.2 = bf16[6,8,64,48,32]{2,3,4,1,0:T(8,128)(2,1)} fusion(bf16[6,8,64,48,32]{2,3,4,1,0:T(8,128)(2,1)} %get-tuple-element.93, s32[]{:T(128)} %get-tuple-element.92, bf16[64,32,1536]{2,0,1:T(8,128)(2,1)} %get-tuple-element.104, bf16[6,8,48,1536]{3,2,1,0:T(8,128)(2,1)} %get-tuple-element.103, s32[]{:T(128)S(6)} %select_n.5), kind=kOutput, calls=%fused_computation.2.clone.1 | convolution fusion | flops 2416705536 | bytes 10617348 | tf_op jit(solution)/shard_map/while/body/eval_jaxpr/acq,bdq->abcd/dot_general | solution.py:25
  138.8 0.6 dynamic_slice.15
  141.1 8.6 %bitcast_dynamic-update-slice_fusion.2 = bf16[6,8,64,48,32]{2,3,4,1,0:T(8,128)(2,1)} fusion(bf16[6,8,64,48,32]{2,3,4,1,0:T(8,128)(2,1)} %get-tuple-element.93, s32[]{:T(128)} %get-tuple-element.92, bf16[64,32,1536]{2,0,1:T(8,128)(2,1)} %get-tuple-element.104, bf16[6,8,48,1536]{3,2,1,0:T(8,128)(2,1)} %get-tuple-element.103, s32[]{:T(128)S(6)} %select_n.5), kind=kOutput, calls=%fused_computation.2.clone.1 | convolution fusion | flops 2416705536 | bytes 10617348 | tf_op jit(solution)/shard_map/while/body/eval_jaxpr/acq,bdq->abcd/dot_general | solution.py:25
  149.7 0.6 dynamic_slice.15
  152.0 8.7 %bitcast_dynamic-update-slice_fusion.2 = bf16[6,8,64,48,32]{2,3,4,1,0:T(8,128)(2,1)} fusion(bf16[6,8,64,48,32]{2,3,4,1,0:T(8,128)(2,1)} %get-tuple-element.93, s32[]{:T(128)} %get-tuple-element.92, bf16[64,32,1536]{2,0,1:T(8,128)(2,1)} %get-tuple-element.104, bf16[6,8,48,1536]{3,2,1,0:T(8,128)(2,1)} %get-tuple-element.103, s32[]{:T(128)S(6)} %select_n.5), kind=kOutput, calls=%fused_computation.2.clone.1 | convolution fusion | flops 2416705536 | bytes 10617348 | tf_op jit(solution)/shard_map/while/body/eval_jaxpr/acq,bdq->abcd/dot_general | solution.py:25
  160.7 0.6 dynamic_slice.15
  163.0 8.7 %bitcast_dynamic-update-slice_fusion.2 = bf16[6,8,64,48,32]{2,3,4,1,0:T(8,128)(2,1)} fusion(bf16[6,8,64,48,32]{2,3,4,1,0:T(8,128)(2,1)} %get-tuple-element.93, s32[]{:T(128)} %get-tuple-element.92, bf16[64,32,1536]{2,0,1:T(8,128)(2,1)} %get-tuple-element.104, bf16[6,8,48,1536]{3,2,1,0:T(8,128)(2,1)} %get-tuple-element.103, s32[]{:T(128)S(6)} %select_n.5), kind=kOutput, calls=%fused_computation.2.clone.1 | convolution fusion | flops 2416705536 | bytes 10617348 | tf_op jit(solution)/shard_map/while/body/eval_jaxpr/acq,bdq->abcd/dot_general | solution.py:25
  171.7 0.6 dynamic_slice.15
  174.0 8.7 %bitcast_dynamic-update-slice_fusion.2 = bf16[6,8,64,48,32]{2,3,4,1,0:T(8,128)(2,1)} fusion(bf16[6,8,64,48,32]{2,3,4,1,0:T(8,128)(2,1)} %get-tuple-element.93, s32[]{:T(128)} %get-tuple-element.92, bf16[64,32,1536]{2,0,1:T(8,128)(2,1)} %get-tuple-element.104, bf16[6,8,48,1536]{3,2,1,0:T(8,128)(2,1)} %get-tuple-element.103, s32[]{:T(128)S(6)} %select_n.5), kind=kOutput, calls=%fused_computation.2.clone.1 | convolution fusion | flops 2416705536 | bytes 10617348 | tf_op jit(solution)/shard_map/while/body/eval_jaxpr/acq,bdq->abcd/dot_general | solution.py:25
  182.7 0.0 all-gather.5.cloned.1.call-done
  182.7 17.6 %convolution_bitcast_fusion = f32[48,64,1024]{2,1,0:T(8,128)} fusion(bf16[48,64,48,32]{1,2,3,0:T(8,128)(2,1)} %bitcast.45, bf16[48,32,1024]{2,0,1:T(8,128)(2,1)} %all-gather.5.cloned.1.call-done), kind=kOutput, calls=%fused_computation.6 | convolution fusion | flops 9663676416 | bytes 25165824 | tf_op jit(solution)/shard_map/abcd,cdo->abo/dot_general | solution.py:30
  200.3 0.0 copy-start.2
  200.3 0.0 copy-start.3
  200.3 0.0 copy-start.1
  200.3 0.0 reduce-scatter.4.cloned.1.call-update
  200.4 0.6 copy-done.2
  201.0 0.0 copy-done.3
  201.0 0.1 broadcast_add_fusion
  201.1 93.2 %reduce-scatter.4.cloned.1.call-done = f32[3,64,1024]{2,1,0:T(8,128)} async-done(((f32[48,64,1024]{2,1,0:T(8,128)}), f32[3,64,1024]{2,1,0:T(8,128)}) %reduce-scatter.4.cloned.1.call-update) | async-done | bytes 786448
  294.3 0.0 copy-done.1
  294.3 1.3 divide_convert_fusion
  295.6 0.0 copy-done
  295.6 2.6 fusion.8
  298.2 0.7 copy.16
  298.9 0.7 reshape.54
  299.7 13.4 %all_to_all.18 = bf16[8,2,12288]{2,1,0:T(2,128)(2,1)} all-to-all(bf16[8,2,12288]{2,1,0:T(2,128)(2,1)S(1)} %reshape.54), channel_id=1, replica_groups=mesh['row'=8,'col'=16] {'row'}, dimensions={0} | all-to-all | bytes 786432 | tf_op jit(solution)/shard_map/all_to_all | solution.py:51
  313.1 1.6 reshape.55
  314.7 1.2 copy.17
  (2 shorter events, 0.0 us)
Async XLA Ops:
  6.5 289.1 %copy-start = (bf16[1024,1024]{1,0:T(8,128)(2,1)S(1)}, bf16[1024,1024]{1,0:T(8,128)(2,1)}, u32[]{:S(2)}) copy-start(bf16[1024,1024]{1,0:T(8,128)(2,1)} %param.17) | copy-start | bytes 6291460
  6.5 90.3 %all-gather.3.cloned.1.call-start = ((), (), s32[]{:S(2)}) async-start(), calls=%async_computation.2 | async-start | bytes 19021824 | tf_op jit(solution)/shard_map/all_gather | solution.py:17
  7.3 175.4 %all-gather.5.cloned.1.call-start = ((), (), s32[]{:S(2)}) async-start(), calls=%async_computation.3 | async-start | bytes 3538944 | tf_op jit(solution)/shard_map/all_gather | solution.py:33
  9.2 285.1 %reduce-scatter.4.cloned.1.call-start = ((), (), s32[]{:S(2)}) async-start(), calls=%async_computation.4 | async-start | bytes 13369344
  200.3 0.7 copy-start.2
  200.3 0.7 copy-start.3
  200.3 94.0 %copy-start.1 = (f32[1024]{0:T(1024)S(1)}, f32[1024]{0:T(1024)}, u32[]{:S(2)}) copy-start(f32[1024]{0:T(1024)} %param.15) | copy-start | bytes 12292
Sparse Core Ops, SparseCore 0:
  10.2 86.5 all-gather.2
  98.5 30.5 all-gather.4
  200.5 93.7 reduce-scatter.3
where the time goes:
time: 323 us; the launch traced here: 322 us
  waiting for transfers between devices  173 us (54%)
  matrix products  72.1 us (22%)
  local copies, waits for them, and re-layouts  39.3 us (12%)
  blocking collectives  13.4 us (4%)
  between operations  13.2 us (4%)
  loops' own time  10.4 us (3%)
    unnamed x4, waiting for transfers between devices  94 us
    all_gather x1, waiting for transfers between devices, local(): window = lax.all_gather(chol_window, ('row', 'col'), axis=2, tiled=True)  78.6 us
    dot_general x6, matrix products, build_tile(): jnp.einsum('acq,bdq->abcd', slab, chol_pairs, preferred_element_type=jnp....  51.9 us
    while x2, local copies, waits for them, and re-layouts, local(): integrals = lax.map(build_tile, jnp.arange(groups, dtype=jnp.int32))  29 us
    dot_general x1, matrix products, local(): jnp.einsum('abcd,cdo->abo', integrals, lax.all_gather(amplitudes, 'row',...  17.6 us
    all_to_all x1, blocking collectives, local(): return lax.all_to_all(mixed, 'row', split_axis=2, concat_axis=1, tiled=True)  13.4 us
    another operation x1, loops' own time, local(): integrals = lax.map(build_tile, jnp.arange(groups, dtype=jnp.int32))  10.4 us
  transfers between devices with their start and end apart: 3, of which 2 were waited for; matrix products, arithmetic and copies ran while one was open for 27% of the time, Pallas kernels for 0%

commit v1 on v0

--- a/solution.py
+++ b/solution.py
@@ -14,7 +14,12 @@
     dress_first,
     dress_second,
 ):
-    window = lax.all_gather(chol_window, ("row", "col"), axis=2, tiled=True)
+    window = jnp.concatenate(
+        lax.all_to_all(
+            jnp.stack([chol_window] * lax.axis_size(("row", "col"))), ("row", "col"), 0, 0
+        ),
+        axis=2,
+    )
     block_b, block_d, aux_count = chol_pairs.shape
     window_size = window.shape[0]
     groups = window_size // 8

time: 323 us -> 411 us (1.27)
  local copies, waits for them, and re-layouts: 39.3 us -> 113 us
  starting transfers between devices: 0.08 us -> 12 us
    all_to_all x0 -> x1, waiting for transfers between devices: none -> 79.1 us  [local(): lax.all_to_all(jnp.stack([chol_window] * lax.axis_size(('row', 'col'))),...]
    all_gather x1 -> x0, waiting for transfers between devices: 78.6 us -> none  [local(): window = lax.all_gather(chol_window, ('row', 'col'), axis=2, tiled=True)]
    unnamed x11 -> x16, local copies, waits for them, and re-layouts: 4.91 us -> 78.5 us
    all_to_all x0 -> x1, starting transfers between devices: none -> 11.9 us  [local(): lax.all_to_all(jnp.stack([chol_window] * lax.axis_size(('row', 'col'))),...]
    unnamed x4 -> x3, waiting for transfers between devices: 94 us -> 94.8 us
  transfers between devices with their start and end apart: 3 -> 3, of which waited for: 2 -> 2; matrix products, arithmetic and copies ran while one was open for 27% -> 28% of each run, Pallas kernels for 0% -> 0%
where the time goes in v1:
time: 411 us; the launch traced here: 409 us
  waiting for transfers between devices  174 us (42%)
  local copies, waits for them, and re-layouts  113 us (27%)
  matrix products  72.1 us (18%)
  between operations  13.5 us (3%)
  blocking collectives  13.4 us (3%)
  starting transfers between devices  12 us (3%)
  loops' own time  10.4 us (3%)
    unnamed x3, waiting for transfers between devices  94.8 us
    all_to_all x1, waiting for transfers between devices, local(): lax.all_to_all(jnp.stack([chol_window] * lax.axis_size(('row', 'col'))),...  79.1 us
    unnamed x16, local copies, waits for them, and re-layouts  78.5 us
    dot_general x6, matrix products, build_tile(): jnp.einsum('acq,bdq->abcd', slab, chol_pairs, preferred_element_type=jnp....  51.9 us
    while x2, local copies, waits for them, and re-layouts, local(): integrals = lax.map(build_tile, jnp.arange(groups, dtype=jnp.int32))  28.9 us
    dot_general x1, matrix products, local(): jnp.einsum('abcd,cdo->abo', integrals, lax.all_gather(amplitudes, 'row',...  17.6 us
    all_to_all x1, blocking collectives, local(): return lax.all_to_all(mixed, 'row', split_axis=2, concat_axis=1, tiled=True)  13.4 us
    all_to_all x1, starting transfers between devices, local(): lax.all_to_all(jnp.stack([chol_window] * lax.axis_size(('row', 'col'))),...  11.9 us
  transfers between devices with their start and end apart: 3, of which 2 were waited for; matrix products, arithmetic and copies ran while one was open for 28% of the time, Pallas kernels for 0%

profile of v1, /device:TPU:1, one launch (start us, length us, event | category | flops | bytes accessed | tf_op | source)
XLA Modules:
  0.0 409.5 jit_solution(11297862932125010521)
XLA Ops:
  6.5 0.0 copy-start
  6.5 8.2 %broadcast_bitcast_fusion = bf16[128,12,48,48]{3,2,1,0:T(8,128)(2,1)} fusion(bf16[48,48,12]{1,0,2:T(8,128)(2,1)} %param.10), kind=kLoop, calls=%fused_computation.13 | loop fusion | bytes 7133184
  14.7 38.3 %reshape.56 = bf16[128,2,13824]{2,1,0:T(2,128)(2,1)} reshape(bf16[128,12,48,48]{3,2,1,0:T(8,128)(2,1)} %broadcast_bitcast_fusion) | data formatting | bytes 14155776
  53.0 0.0 copy-start.1
  53.0 11.9 %all-to-all-start = ((bf16[128,2,13824]{2,1,0:T(2,128)(2,1)}), bf16[128,2,13824]{2,1,0:T(2,128)(2,1)}, u32[]{:S(2)}, u32[]{:S(2)}) async-start(bf16[128,2,13824]{2,1,0:T(2,128)(2,1)} %reshape.56), calls=%async_computation | async-start | bytes 14155776 | tf_op jit(solution)/shard_map/all_to_all | solution.py:18
  64.9 0.0 all-gather.2.cloned.1.call-start
  65.0 0.0 copy-done.1
  65.0 0.9 copy.19
  65.9 0.0 all-gather.2.cloned.1.call-update
  65.9 0.0 reduce-scatter.4.cloned.1.call-start
  65.9 8.9 %copy.18 = bf16[64,32,1536]{2,0,1:T(8,128)(2,1)} copy(bf16[64,32,1536]{2,1,0:T(8,128)(2,1)} %param.11) | data formatting | bytes 12582912 | tf_op jit(solution)/shard_map/while | solution.py:33
  74.8 79.1 %all-to-all-done = bf16[128,2,13824]{2,1,0:T(2,128)(2,1)} async-done(((bf16[128,2,13824]{2,1,0:T(2,128)(2,1)}), bf16[128,2,13824]{2,1,0:T(2,128)(2,1)}, u32[]{:S(2)}, u32[]{:S(2)}) %all-to-all-start) | async-done | bytes 7077920 | tf_op jit(solution)/shard_map/all_to_all | solution.py:18
  153.9 28.1 %reshape.57 = bf16[128,12,48,48]{3,2,1,0:T(8,128)(2,1)} reshape(bf16[128,2,13824]{2,1,0:T(2,128)(2,1)} %all-to-all-done) | data formatting | bytes 14155776
  182.1 20.0 %copy.17 = bf16[6,8,48,1536]{3,2,1,0:T(8,128)(2,1)} copy(bf16[6,8,48,1536]{2,1,0,3:T(8,128)(2,1)} %bitcast.50) | data formatting | bytes 14155776 | tf_op jit(solution)/shard_map/while | solution.py:33
  202.0 65.8 %while.10 = (s32[]{:T(128)}, bf16[6,8,64,48,32]{2,3,4,1,0:T(8,128)(2,1)}, s32[6]{0:T(128)S(1)}, bf16[6,8,48,1536]{3,2,1,0:T(8,128)(2,1)}, bf16[64,32,1536]{2,0,1...) while((s32[]{:T(128)}, bf16[6,8,64,48,32]{2,3,4,1,0:T(8,128)(2,1)}, s32[6]{0:T(128)S(1)}, ...), condition=%wide.region_1.2_spmd, body=%wide.region_0.1_spmd.sunk | while | flops 2416705536 | bytes 10617479 | solution.py:33
  202.0 0.6 dynamic_slice.15
  204.4 8.6 %bitcast_dynamic-update-slice_fusion.2 = bf16[6,8,64,48,32]{2,3,4,1,0:T(8,128)(2,1)} fusion(bf16[6,8,64,48,32]{2,3,4,1,0:T(8,128)(2,1)} %get-tuple-element.98, s32[]{:T(128)} %get-tuple-element.97, bf16[64,32,1536]{2,0,1:T(8,128)(2,1)} %get-tuple-element.109, bf16[6,8,48,1536]{3,2,1,0:T(8,128)(2,1)} %get-tuple-element.108, s32[]{:T(128)S(6)} %select_n.5), kind=kOutput, calls=%fused_computation.2.clone.1 | convolution fusion | flops 2416705536 | bytes 10617348 | tf_op jit(solution)/shard_map/while/body/eval_jaxpr/acq,bdq->abcd/dot_general | solution.py:30
  213.0 0.6 dynamic_slice.15
  215.3 8.6 %bitcast_dynamic-update-slice_fusion.2 = bf16[6,8,64,48,32]{2,3,4,1,0:T(8,128)(2,1)} fusion(bf16[6,8,64,48,32]{2,3,4,1,0:T(8,128)(2,1)} %get-tuple-element.98, s32[]{:T(128)} %get-tuple-element.97, bf16[64,32,1536]{2,0,1:T(8,128)(2,1)} %get-tuple-element.109, bf16[6,8,48,1536]{3,2,1,0:T(8,128)(2,1)} %get-tuple-element.108, s32[]{:T(128)S(6)} %select_n.5), kind=kOutput, calls=%fused_computation.2.clone.1 | convolution fusion | flops 2416705536 | bytes 10617348 | tf_op jit(solution)/shard_map/while/body/eval_jaxpr/acq,bdq->abcd/dot_general | solution.py:30
  223.9 0.6 dynamic_slice.15
  226.3 8.6 %bitcast_dynamic-update-slice_fusion.2 = bf16[6,8,64,48,32]{2,3,4,1,0:T(8,128)(2,1)} fusion(bf16[6,8,64,48,32]{2,3,4,1,0:T(8,128)(2,1)} %get-tuple-element.98, s32[]{:T(128)} %get-tuple-element.97, bf16[64,32,1536]{2,0,1:T(8,128)(2,1)} %get-tuple-element.109, bf16[6,8,48,1536]{3,2,1,0:T(8,128)(2,1)} %get-tuple-element.108, s32[]{:T(128)S(6)} %select_n.5), kind=kOutput, calls=%fused_computation.2.clone.1 | convolution fusion | flops 2416705536 | bytes 10617348 | tf_op jit(solution)/shard_map/while/body/eval_jaxpr/acq,bdq->abcd/dot_general | solution.py:30
  234.9 0.6 dynamic_slice.15
  237.2 8.7 %bitcast_dynamic-update-slice_fusion.2 = bf16[6,8,64,48,32]{2,3,4,1,0:T(8,128)(2,1)} fusion(bf16[6,8,64,48,32]{2,3,4,1,0:T(8,128)(2,1)} %get-tuple-element.98, s32[]{:T(128)} %get-tuple-element.97, bf16[64,32,1536]{2,0,1:T(8,128)(2,1)} %get-tuple-element.109, bf16[6,8,48,1536]{3,2,1,0:T(8,128)(2,1)} %get-tuple-element.108, s32[]{:T(128)S(6)} %select_n.5), kind=kOutput, calls=%fused_computation.2.clone.1 | convolution fusion | flops 2416705536 | bytes 10617348 | tf_op jit(solution)/shard_map/while/body/eval_jaxpr/acq,bdq->abcd/dot_general | solution.py:30
  245.9 0.6 dynamic_slice.15
  248.2 8.7 %bitcast_dynamic-update-slice_fusion.2 = bf16[6,8,64,48,32]{2,3,4,1,0:T(8,128)(2,1)} fusion(bf16[6,8,64,48,32]{2,3,4,1,0:T(8,128)(2,1)} %get-tuple-element.98, s32[]{:T(128)} %get-tuple-element.97, bf16[64,32,1536]{2,0,1:T(8,128)(2,1)} %get-tuple-element.109, bf16[6,8,48,1536]{3,2,1,0:T(8,128)(2,1)} %get-tuple-element.108, s32[]{:T(128)S(6)} %select_n.5), kind=kOutput, calls=%fused_computation.2.clone.1 | convolution fusion | flops 2416705536 | bytes 10617348 | tf_op jit(solution)/shard_map/while/body/eval_jaxpr/acq,bdq->abcd/dot_general | solution.py:30
  256.8 0.6 dynamic_slice.15
  259.1 8.7 %bitcast_dynamic-update-slice_fusion.2 = bf16[6,8,64,48,32]{2,3,4,1,0:T(8,128)(2,1)} fusion(bf16[6,8,64,48,32]{2,3,4,1,0:T(8,128)(2,1)} %get-tuple-element.98, s32[]{:T(128)} %get-tuple-element.97, bf16[64,32,1536]{2,0,1:T(8,128)(2,1)} %get-tuple-element.109, bf16[6,8,48,1536]{3,2,1,0:T(8,128)(2,1)} %get-tuple-element.108, s32[]{:T(128)S(6)} %select_n.5), kind=kOutput, calls=%fused_computation.2.clone.1 | convolution fusion | flops 2416705536 | bytes 10617348 | tf_op jit(solution)/shard_map/while/body/eval_jaxpr/acq,bdq->abcd/dot_general | solution.py:30
  267.8 0.0 all-gather.2.cloned.1.call-done
  267.8 17.6 %convolution_bitcast_fusion = f32[48,64,1024]{2,1,0:T(8,128)} fusion(bf16[48,64,48,32]{1,2,3,0:T(8,128)(2,1)} %bitcast.51, bf16[48,32,1024]{2,0,1:T(8,128)(2,1)} %all-gather.2.cloned.1.call-done), kind=kOutput, calls=%fused_computation.6 | convolution fusion | flops 9663676416 | bytes 25165824 | tf_op jit(solution)/shard_map/abcd,cdo->abo/dot_general | solution.py:35
  285.5 0.0 copy-start.3
  285.5 0.0 copy-start.4
  285.5 0.0 copy-start.2
  285.5 0.0 reduce-scatter.4.cloned.1.call-update
  285.5 0.6 copy-done.3
  286.1 0.0 copy-done.4
  286.2 0.1 broadcast_add_fusion
  286.2 94.8 %reduce-scatter.4.cloned.1.call-done = f32[3,64,1024]{2,1,0:T(8,128)} async-done(((f32[48,64,1024]{2,1,0:T(8,128)}), f32[3,64,1024]{2,1,0:T(8,128)}) %reduce-scatter.4.cloned.1.call-update) | async-done | bytes 786448
  381.0 0.0 copy-done.2
  381.0 1.3 divide_convert_fusion
  382.3 0.0 copy-done
  382.3 2.6 fusion.8
  384.9 0.7 copy.20
  385.6 0.7 reshape.58
  386.4 13.4 %all_to_all.23 = bf16[8,2,12288]{2,1,0:T(2,128)(2,1)} all-to-all(bf16[8,2,12288]{2,1,0:T(2,128)(2,1)S(1)} %reshape.58), channel_id=1, replica_groups=mesh['row'=8,'col'=16] {'row'}, dimensions={0} | all-to-all | bytes 786432 | tf_op jit(solution)/shard_map/all_to_all | solution.py:56
  399.8 1.6 reshape.59
  401.4 1.2 copy.21
  (2 shorter events, 0.0 us)
Async XLA Ops:
  6.5 375.8 %copy-start = (bf16[1024,1024]{1,0:T(8,128)(2,1)S(1)}, bf16[1024,1024]{1,0:T(8,128)(2,1)}, u32[]{:S(2)}) copy-start(bf16[1024,1024]{1,0:T(8,128)(2,1)} %param.17) | copy-start | bytes 6291460
  53.0 11.9 %copy-start.1 = (bf16[48,32,128]{2,1,0:T(8,128)(2,1)S(1)}, bf16[48,32,128]{2,1,0:T(8,128)(2,1)}, u32[]{:S(2)}) copy-start(bf16[48,32,128]{2,1,0:T(8,128)(2,1)} %param.12) | copy-start | bytes 1179652
  53.0 100.9 %all-to-all-start = ((bf16[128,2,13824]{2,1,0:T(2,128)(2,1)}), bf16[128,2,13824]{2,1,0:T(2,128)(2,1)}, u32[]{:S(2)}, u32[]{:S(2)}) async-start(bf16[128,2,13824]{2,1,0:T(2,128)(2,1)} %reshape.56), calls=%async_computation | async-start | bytes 14155776 | tf_op jit(solution)/shard_map/all_to_all | solution.py:18
  64.9 202.9 %all-gather.2.cloned.1.call-start = ((), (), s32[]{:S(2)}) async-start(), calls=%async_computation.3 | async-start | bytes 3538944 | tf_op jit(solution)/shard_map/all_gather | solution.py:38
  65.9 315.1 %reduce-scatter.4.cloned.1.call-start = ((), (), s32[]{:S(2)}) async-start(), calls=%async_computation.4 | async-start | bytes 13369344
  285.5 0.7 copy-start.3
  285.5 0.7 copy-start.4
  285.5 95.5 %copy-start.2 = (f32[1024]{0:T(1024)S(1)}, f32[1024]{0:T(1024)}, u32[]{:S(2)}) copy-start(f32[1024]{0:T(1024)} %param.15) | copy-start | bytes 12292
Sparse Core Ops, SparseCore 0:
  67.4 93.0 all-gather.1
  285.6 95.3 reduce-scatter.3
